TPU v7x, 512 devices: a whole 4x4x16 slice. The times are simulated.
512 devices in a mesh: row: 16 (over y, x), col: 32 (over z, core).
Axes of the slice: x: 4, y: 4, z: 16, core: 2. Of those that a mesh axis runs over, the one named last changes fastest.
Arguments:
- sources: bfloat16 [131072, 1024], P(('row', 'col')), may hold values from -6 to 6
- leaf_in: bfloat16 [512, 256, 256], P(('row', 'col')), may hold values from -0.375 to 0.375
- transfers: bfloat16 [512, 9, 2, 256, 256], P(('row', 'col')), may hold values from -0.25 to 0.25
- leaf_out: bfloat16 [512, 256, 256], P(('row', 'col')), may hold values from -0.375 to 0.375
- tile_mats: bfloat16 [512, 5, 256, 256], P(('row', 'col')), may hold values from -0.375 to 0.375
- tile_list: int32 [512, 5], P(('row', 'col')), may hold values from 0 to 1, as said below
Outputs:
- applied: bfloat16 [131072, 1024], P(('row', 'col'))
Inputs may be any that keep to these rules, and one draw needn't show every extreme that they name: tile_list[b, k] is 1 where source block b holds a tile onto the block k - 2 places further along its row of 32 blocks; always 1 for k = 2, always 0 where that block lies outside the row; blocks hold different numbers of tiles.
All inputs are finite; a program needn't handle non-finite values.
Results may differ from a plain program's by a relative error of at most 0.015.
Values may be sent and summed in bfloat16 or wider, within the bound.
No kernel may reach another device: no remote copies, remote signals or barrier semaphores. Data moves between devices by JAX's collectives and lax.ppermute only.
A program may use at most 64 MiB of HBM per device.

v0:
```python
import jax
import jax.numpy as jnp
from jax import lax
from jax.sharding import PartitionSpec as P

TILES = 5


def from_partner(block, axis, apart):
    count = lax.axis_size(axis)
    route = []
    for low in range(count):
        high = low | 1 << apart
        if high != low and high < count:
            route += [(low, high), (high, low)]
    return lax.ppermute(block, axis, route)


def from_behind(shard, axis, by):
    devices = lax.axis_size(axis)
    pairs = [(i, i + by) for i in range(devices) if 0 <= i + by < devices]
    return lax.ppermute(shard, axis, pairs)


def mixing(mats, vectors):
    return jnp.dot(mats, vectors, preferred_element_type=jnp.float32)


def shards(sources, leaf_in, transfers, leaf_out, tile_mats, tile_list):
    coeffs = mixing(leaf_in[0], sources).astype(jnp.bfloat16)
    levels_high = lax.axis_size("row").bit_length() - 1
    levels_low = lax.axis_size("col").bit_length() - 1
    for bit in range(levels_high):
        partner = from_partner(coeffs, "row", bit)
        coeffs = (
            mixing(transfers[0, bit, 0], coeffs) + mixing(transfers[0, bit, 1], partner)
        ).astype(jnp.bfloat16)
    for bit in range(levels_low):
        level = levels_high + bit
        partner = from_partner(coeffs, "col", bit)
        coeffs = (
            mixing(transfers[0, level, 0], coeffs) + mixing(transfers[0, level, 1], partner)
        ).astype(jnp.bfloat16)
    far = mixing(leaf_out[0], coeffs)
    live = tile_list[0].astype(jnp.float32)
    middle = TILES // 2
    near = live[middle] * mixing(tile_mats[0, middle], sources)
    for k in range(TILES):
        if k == middle:
            continue
        product = live[k] * mixing(tile_mats[0, k], sources)
        near = near + from_behind(product.astype(jnp.bfloat16), "col", k - middle).astype(
            product.dtype
        )
    return (far + near).astype(jnp.bfloat16)


def solution(mesh):
    return jax.shard_map(
        shards,
        mesh=mesh,
        in_specs=(
            P(("row", "col"), None),
            P(("row", "col"), None, None),
            P(("row", "col"), None, None, None, None),
            P(("row", "col"), None, None),
            P(("row", "col"), None, None, None),
            P(("row", "col"), None),
        ),
        out_specs=P(("row", "col"), None),
        check_vma=False,
    )
```

profile of v0, /device:TPU:96, one launch (start us, length us, event | category | flops | bytes accessed | tf_op | source)
XLA Modules:
  0.0 225.2 jit_solution(15803876884940158773)
XLA Ops:
  0.0 0.0 copy-start
  0.0 0.0 copy-start.1
  0.0 1.0 copy-done
  1.0 1.2 convolution_convert_fusion
  2.3 3.4 %collective-permute-start = (bf16[256,1024]{1,0:T(8,128)(2,1)S(1)}, bf16[256,1024]{1,0:T(8,128)(2,1)S(1)}, u32[]{:S(2)}, u32[]{:S(2)}) collective-permute-start(bf16[256,1024]{1,0:T(8,128)(2,1)S(1)} %convolution_convert_fusion), channel_id=1, source_target_pairs={{0,32},{32,0},{64,96},{96,64},{128,160},{160,128},{192,224},{224,1... | collective-permute-start | bytes 1572872 | tf_op jit(solution)/shard_map/ppermute | solution.py:16
  5.7 1.3 fusion.47
  6.9 10.9 %collective-permute-done = bf16[256,1024]{1,0:T(8,128)(2,1)S(1)} collective-permute-done((bf16[256,1024]{1,0:T(8,128)(2,1)S(1)}, bf16[256,1024]{1,0:T(8,128)(2,1)S(1)}, u32[]{:S(2)}, u32[]{:S(2)}) %collective-permute-start) | collective-permute-done | bytes 524320 | tf_op jit(solution)/shard_map/ppermute | solution.py:16
  17.8 0.0 copy-done.1
  17.8 0.4 fusion
  18.2 4.9 %collective-permute-start.1 = (bf16[256,1024]{0,1:T(8,128)(2,1)S(1)}, bf16[256,1024]{0,1:T(8,128)(2,1)S(1)}, u32[]{:S(2)}, u32[]{:S(2)}) collective-permute-start(bf16[256,1024]{0,1:T(8,128)(2,1)S(1)} %bitcast.123), channel_id=1, source_target_pairs={{0,64},{64,0},{32,96},{96,32},{128,192},{192,128},{160,224},{224,1... | collective-permute-start | bytes 1572872 | tf_op jit(solution)/shard_map/ppermute | solution.py:16
  23.1 0.3 fusion.44
  23.4 10.9 %collective-permute-done.1 = bf16[256,1024]{0,1:T(8,128)(2,1)S(1)} collective-permute-done((bf16[256,1024]{0,1:T(8,128)(2,1)S(1)}, bf16[256,1024]{0,1:T(8,128)(2,1)S(1)}, u32[]{:S(2)}, u32[]{:S(2)}) %collective-permute-start.1) | collective-permute-done | bytes 524320 | tf_op jit(solution)/shard_map/ppermute | solution.py:16
  34.4 0.3 fusion.1
  34.7 3.5 %collective-permute-start.2 = (bf16[256,1024]{0,1:T(8,128)(2,1)S(1)}, bf16[256,1024]{0,1:T(8,128)(2,1)S(1)}, u32[]{:S(2)}, u32[]{:S(2)}) collective-permute-start(bf16[256,1024]{0,1:T(8,128)(2,1)S(1)} %bitcast.124), channel_id=1, source_target_pairs={{0,128},{128,0},{32,160},{160,32},{64,192},{192,64},{96,224},{224,... | collective-permute-start | bytes 1572872 | tf_op jit(solution)/shard_map/ppermute | solution.py:16
  38.2 0.3 fusion.41
  38.5 10.0 %collective-permute-done.2 = bf16[256,1024]{0,1:T(8,128)(2,1)S(1)} collective-permute-done((bf16[256,1024]{0,1:T(8,128)(2,1)S(1)}, bf16[256,1024]{0,1:T(8,128)(2,1)S(1)}, u32[]{:S(2)}, u32[]{:S(2)}) %collective-permute-start.2) | collective-permute-done | bytes 524320 | tf_op jit(solution)/shard_map/ppermute | solution.py:16
  48.6 0.3 fusion.2
  48.9 5.1 %collective-permute-start.3 = (bf16[256,1024]{0,1:T(8,128)(2,1)S(1)}, bf16[256,1024]{0,1:T(8,128)(2,1)S(1)}, u32[]{:S(2)}, u32[]{:S(2)}) collective-permute-start(bf16[256,1024]{0,1:T(8,128)(2,1)S(1)} %bitcast.125), channel_id=1, source_target_pairs={{0,256},{256,0},{32,288},{288,32},{64,320},{320,64},{96,352},{352,... | collective-permute-start | bytes 1572872 | tf_op jit(solution)/shard_map/ppermute | solution.py:16
  54.0 0.3 fusion.38
  54.3 9.0 %collective-permute-done.3 = bf16[256,1024]{0,1:T(8,128)(2,1)S(1)} collective-permute-done((bf16[256,1024]{0,1:T(8,128)(2,1)S(1)}, bf16[256,1024]{0,1:T(8,128)(2,1)S(1)}, u32[]{:S(2)}, u32[]{:S(2)}) %collective-permute-start.3) | collective-permute-done | bytes 524320 | tf_op jit(solution)/shard_map/ppermute | solution.py:16
  63.4 0.3 fusion.3
  63.7 0.0 copy-start.5
  63.7 1.9 collective-permute-start.4
  65.7 0.3 fusion.35
  66.0 1.5 collective-permute-done.4
  67.5 0.3 fusion.4
  67.9 0.0 copy-start.2
  67.9 2.2 collective-permute-start.5
  70.0 0.0 copy-done.5
  70.1 0.7 fusion.74
  70.7 0.3 fusion.32
  71.1 12.8 %collective-permute-done.5 = bf16[256,1024]{0,1:T(8,128)(2,1)S(1)} collective-permute-done((bf16[256,1024]{0,1:T(8,128)(2,1)S(1)}, bf16[256,1024]{0,1:T(8,128)(2,1)S(1)}, u32[]{:S(2)}, u32[]{:S(2)}) %collective-permute-start.5) | collective-permute-done | bytes 524320 | tf_op jit(solution)/shard_map/ppermute | solution.py:16
  83.9 0.3 fusion.5
  84.2 1.9 collective-permute-start.6
  86.1 0.0 copy-done.2
  86.1 1.0 fusion.10
  87.1 1.9 collective-permute-start.10
  89.0 1.0 fusion.11
  90.0 2.4 %collective-permute-start.11 = (bf16[256,1024]{0,1:T(8,128)(2,1)S(1)}, bf16[256,1024]{0,1:T(8,128)(2,1)}, u32[]{:S(2)}, u32[]{:S(2)}) collective-permute-start(bf16[256,1024]{0,1:T(8,128)(2,1)S(1)} %fusion.11), channel_id=1, source_target_pairs={{0,1},{1,2},{2,3},{3,4},{4,5},{5,6},{6,7},{7,8},{8,9},{9,10},{10,1... | collective-permute-start | bytes 1572872 | tf_op jit(solution)/shard_map/ppermute | solution.py:22
  92.4 0.3 fusion.29
  92.8 18.6 %collective-permute-done.6 = bf16[256,1024]{0,1:T(8,128)(2,1)S(1)} collective-permute-done((bf16[256,1024]{0,1:T(8,128)(2,1)S(1)}, bf16[256,1024]{0,1:T(8,128)(2,1)S(1)}, u32[]{:S(2)}, u32[]{:S(2)}) %collective-permute-start.6) | collective-permute-done | bytes 524320 | tf_op jit(solution)/shard_map/ppermute | solution.py:16
  111.4 0.3 fusion.6
  111.7 9.1 %collective-permute-start.7 = (bf16[256,1024]{0,1:T(8,128)(2,1)S(1)}, bf16[256,1024]{0,1:T(8,128)(2,1)S(1)}, u32[]{:S(2)}, u32[]{:S(2)}) collective-permute-start(bf16[256,1024]{0,1:T(8,128)(2,1)S(1)} %bitcast.121), channel_id=1, source_target_pairs={{0,8},{8,0},{1,9},{9,1},{2,10},{10,2},{3,11},{11,3},{4,12},{12,4},... | collective-permute-start | bytes 1572872 | tf_op jit(solution)/shard_map/ppermute | solution.py:16
  120.8 1.0 fusion.12
  121.8 1.9 collective-permute-start.12
  123.7 1.0 fusion.9
  124.7 3.9 %collective-permute-start.9 = (bf16[256,1024]{0,1:T(8,128)(2,1)S(1)}, bf16[256,1024]{0,1:T(8,128)(2,1)S(1)}, u32[]{:S(2)}, u32[]{:S(2)}) collective-permute-start(bf16[256,1024]{0,1:T(8,128)(2,1)S(1)} %fusion.9), channel_id=1, source_target_pairs={{2,0},{3,1},{4,2},{5,3},{6,4},{7,5},{8,6},{9,7},{10,8},{11,9},{12,... | collective-permute-start | bytes 1572872 | tf_op jit(solution)/shard_map/ppermute | solution.py:22
  128.7 0.3 fusion.26
  129.0 0.0 copy-start.4
  129.0 34.3 %collective-permute-done.7 = bf16[256,1024]{0,1:T(8,128)(2,1)S(1)} collective-permute-done((bf16[256,1024]{0,1:T(8,128)(2,1)S(1)}, bf16[256,1024]{0,1:T(8,128)(2,1)S(1)}, u32[]{:S(2)}, u32[]{:S(2)}) %collective-permute-start.7) | collective-permute-done | bytes 524320 | tf_op jit(solution)/shard_map/ppermute | solution.py:16
  163.3 0.3 fusion.7
  163.6 10.1 %collective-permute-start.8 = (bf16[256,1024]{0,1:T(8,128)(2,1)S(1)}, bf16[256,1024]{0,1:T(8,128)(2,1)}, u32[]{:S(2)}, u32[]{:S(2)}) collective-permute-start(bf16[256,1024]{0,1:T(8,128)(2,1)S(1)} %bitcast.119), channel_id=1, source_target_pairs={{0,16},{16,0},{1,17},{17,1},{2,18},{18,2},{3,19},{19,3},{4,20},{20... | collective-permute-start | bytes 1572872 | tf_op jit(solution)/shard_map/ppermute | solution.py:16
  173.7 1.0 convolution_multiply_fusion.4
  174.7 0.3 fusion.23
  175.0 0.0 collective-permute-done.10
  175.1 0.0 collective-permute-done.11
  175.1 42.8 %collective-permute-done.12 = bf16[256,1024]{0,1:T(8,128)(2,1)} collective-permute-done((bf16[256,1024]{0,1:T(8,128)(2,1)S(1)}, bf16[256,1024]{0,1:T(8,128)(2,1)}, u32[]{:S(2)}, u32[]{:S(2)}) %collective-permute-start.12) | collective-permute-done | bytes 524320 | tf_op jit(solution)/shard_map/ppermute | solution.py:22
  217.9 0.0 collective-permute-done.9
  217.9 0.0 copy-start.3
  217.9 0.8 copy-done.3
  218.7 3.2 %collective-permute-done.8 = bf16[256,1024]{0,1:T(8,128)(2,1)} collective-permute-done((bf16[256,1024]{0,1:T(8,128)(2,1)S(1)}, bf16[256,1024]{0,1:T(8,128)(2,1)}, u32[]{:S(2)}, u32[]{:S(2)}) %collective-permute-start.8) | collective-permute-done | bytes 524320 | tf_op jit(solution)/shard_map/ppermute | solution.py:16
  221.9 0.0 copy-done.4
  221.9 2.3 %fusion.14 = bf16[256,1024]{0,1:T(8,128)(2,1)S(1)} fusion(f32[1024,256]{1,0:T(8,128)S(1)} %fusion.23, bf16[256,1024]{0,1:T(8,128)(2,1)} %collective-permute-done.8, bf16[256,1024]{0,1:T(8,128)(2,1)} %collective-permute-done.12, bf16[256,1024]{0,1:T(8,128)(2,1)} %collective-permute-done.11, bf16[256,1024]{0,1:T(8,128)(2,1)} %collective-permute-done.10, ...), kind=kOutput, calls=%fused_computation.30 | convolution fusion | flops 271581184 | bytes 5505024 | tf_op jit(solution)/shard_map/dot_general | solution.py:26
  224.2 1.0 copy.12
  (1 shorter events, 0.0 us)
Async XLA Ops:
  0.0 1.0 copy-start
  0.0 17.8 %copy-start.1 = (bf16[1,9,2,256,256]{4,3,2,1,0:T(8,128)(2,1)S(1)}, bf16[1,9,2,256,256]{4,3,2,1,0:T(8,128)(2,1)}, u32[]{:S(2)}) copy-start(bf16[1,9,2,256,256]{4,3,2,1,0:T(8,128)(2,1)} %param.8) | copy-start | bytes 7077892
  2.3 15.6 %collective-permute-start = (bf16[256,1024]{1,0:T(8,128)(2,1)S(1)}, bf16[256,1024]{1,0:T(8,128)(2,1)S(1)}, u32[]{:S(2)}, u32[]{:S(2)}) collective-permute-start(bf16[256,1024]{1,0:T(8,128)(2,1)S(1)} %convolution_convert_fusion), channel_id=1, source_target_pairs={{0,32},{32,0},{64,96},{96,64},{128,160},{160,128},{192,224},{224,1... | collective-permute-start | bytes 1572872 | tf_op jit(solution)/shard_map/ppermute | solution.py:16
  18.2 16.2 %collective-permute-start.1 = (bf16[256,1024]{0,1:T(8,128)(2,1)S(1)}, bf16[256,1024]{0,1:T(8,128)(2,1)S(1)}, u32[]{:S(2)}, u32[]{:S(2)}) collective-permute-start(bf16[256,1024]{0,1:T(8,128)(2,1)S(1)} %bitcast.123), channel_id=1, source_target_pairs={{0,64},{64,0},{32,96},{96,32},{128,192},{192,128},{160,224},{224,1... | collective-permute-start | bytes 1572872 | tf_op jit(solution)/shard_map/ppermute | solution.py:16
  34.7 13.8 %collective-permute-start.2 = (bf16[256,1024]{0,1:T(8,128)(2,1)S(1)}, bf16[256,1024]{0,1:T(8,128)(2,1)S(1)}, u32[]{:S(2)}, u32[]{:S(2)}) collective-permute-start(bf16[256,1024]{0,1:T(8,128)(2,1)S(1)} %bitcast.124), channel_id=1, source_target_pairs={{0,128},{128,0},{32,160},{160,32},{64,192},{192,64},{96,224},{224,... | collective-permute-start | bytes 1572872 | tf_op jit(solution)/shard_map/ppermute | solution.py:16
  48.9 14.5 %collective-permute-start.3 = (bf16[256,1024]{0,1:T(8,128)(2,1)S(1)}, bf16[256,1024]{0,1:T(8,128)(2,1)S(1)}, u32[]{:S(2)}, u32[]{:S(2)}) collective-permute-start(bf16[256,1024]{0,1:T(8,128)(2,1)S(1)} %bitcast.125), channel_id=1, source_target_pairs={{0,256},{256,0},{32,288},{288,32},{64,320},{320,64},{96,352},{352,... | collective-permute-start | bytes 1572872 | tf_op jit(solution)/shard_map/ppermute | solution.py:16
  63.7 6.3 %copy-start.5 = (s32[1,5]{1,0:T(1,128)S(1)}, s32[1,5]{1,0:T(1,128)}, u32[]{:S(2)}) copy-start(s32[1,5]{1,0:T(1,128)} %param.11) | copy-start | bytes 64
  63.7 3.8 %collective-permute-start.4 = (bf16[256,1024]{0,1:T(8,128)(2,1)S(1)}, bf16[256,1024]{0,1:T(8,128)(2,1)S(1)}, u32[]{:S(2)}, u32[]{:S(2)}) collective-permute-start(bf16[256,1024]{0,1:T(8,128)(2,1)S(1)} %bitcast.126), channel_id=1, source_target_pairs={{0,1},{1,0},{2,3},{3,2},{4,5},{5,4},{6,7},{7,6},{8,9},{9,8},{10,11... | collective-permute-start | bytes 1572872 | tf_op jit(solution)/shard_map/ppermute | solution.py:16
  67.9 18.3 %copy-start.2 = (bf16[1,5,256,256]{3,2,1,0:T(8,128)(2,1)S(1)}, bf16[1,5,256,256]{3,2,1,0:T(8,128)(2,1)}, u32[]{:S(2)}) copy-start(bf16[1,5,256,256]{3,2,1,0:T(8,128)(2,1)} %param.10) | copy-start | bytes 1966084
  67.9 16.0 %collective-permute-start.5 = (bf16[256,1024]{0,1:T(8,128)(2,1)S(1)}, bf16[256,1024]{0,1:T(8,128)(2,1)S(1)}, u32[]{:S(2)}, u32[]{:S(2)}) collective-permute-start(bf16[256,1024]{0,1:T(8,128)(2,1)S(1)} %bitcast.122), channel_id=1, source_target_pairs={{0,2},{2,0},{1,3},{3,1},{4,6},{6,4},{5,7},{7,5},{8,10},{10,8},{9,1... | collective-permute-start | bytes 1572872 | tf_op jit(solution)/shard_map/ppermute | solution.py:16
  84.2 27.2 %collective-permute-start.6 = (bf16[256,1024]{0,1:T(8,128)(2,1)S(1)}, bf16[256,1024]{0,1:T(8,128)(2,1)S(1)}, u32[]{:S(2)}, u32[]{:S(2)}) collective-permute-start(bf16[256,1024]{0,1:T(8,128)(2,1)S(1)} %bitcast.120), channel_id=1, source_target_pairs={{0,4},{4,0},{1,5},{5,1},{2,6},{6,2},{3,7},{7,3},{8,12},{12,8},{9,1... | collective-permute-start | bytes 1572872 | tf_op jit(solution)/shard_map/ppermute | solution.py:16
  87.1 87.9 %collective-permute-start.10 = (bf16[256,1024]{0,1:T(8,128)(2,1)S(1)}, bf16[256,1024]{0,1:T(8,128)(2,1)}, u32[]{:S(2)}, u32[]{:S(2)}) collective-permute-start(bf16[256,1024]{0,1:T(8,128)(2,1)S(1)} %fusion.10), channel_id=1, source_target_pairs={{1,0},{2,1},{3,2},{4,3},{5,4},{6,5},{7,6},{8,7},{9,8},{10,9},{11,1... | collective-permute-start | bytes 1572872 | tf_op jit(solution)/shard_map/ppermute | solution.py:22
  90.0 85.0 %collective-permute-start.11 = (bf16[256,1024]{0,1:T(8,128)(2,1)S(1)}, bf16[256,1024]{0,1:T(8,128)(2,1)}, u32[]{:S(2)}, u32[]{:S(2)}) collective-permute-start(bf16[256,1024]{0,1:T(8,128)(2,1)S(1)} %fusion.11), channel_id=1, source_target_pairs={{0,1},{1,2},{2,3},{3,4},{4,5},{5,6},{6,7},{7,8},{8,9},{9,10},{10,1... | collective-permute-start | bytes 1572872 | tf_op jit(solution)/shard_map/ppermute | solution.py:22
  111.7 51.5 %collective-permute-start.7 = (bf16[256,1024]{0,1:T(8,128)(2,1)S(1)}, bf16[256,1024]{0,1:T(8,128)(2,1)S(1)}, u32[]{:S(2)}, u32[]{:S(2)}) collective-permute-start(bf16[256,1024]{0,1:T(8,128)(2,1)S(1)} %bitcast.121), channel_id=1, source_target_pairs={{0,8},{8,0},{1,9},{9,1},{2,10},{10,2},{3,11},{11,3},{4,12},{12,4},... | collective-permute-start | bytes 1572872 | tf_op jit(solution)/shard_map/ppermute | solution.py:16
  121.8 96.1 %collective-permute-start.12 = (bf16[256,1024]{0,1:T(8,128)(2,1)S(1)}, bf16[256,1024]{0,1:T(8,128)(2,1)}, u32[]{:S(2)}, u32[]{:S(2)}) collective-permute-start(bf16[256,1024]{0,1:T(8,128)(2,1)S(1)} %fusion.12), channel_id=1, source_target_pairs={{0,2},{1,3},{2,4},{3,5},{4,6},{5,7},{6,8},{7,9},{8,10},{9,11},{10,... | collective-permute-start | bytes 1572872 | tf_op jit(solution)/shard_map/ppermute | solution.py:22
  124.7 93.1 %collective-permute-start.9 = (bf16[256,1024]{0,1:T(8,128)(2,1)S(1)}, bf16[256,1024]{0,1:T(8,128)(2,1)S(1)}, u32[]{:S(2)}, u32[]{:S(2)}) collective-permute-start(bf16[256,1024]{0,1:T(8,128)(2,1)S(1)} %fusion.9), channel_id=1, source_target_pairs={{2,0},{3,1},{4,2},{5,3},{6,4},{7,5},{8,6},{9,7},{10,8},{11,9},{12,... | collective-permute-start | bytes 1572872 | tf_op jit(solution)/shard_map/ppermute | solution.py:22
  129.0 92.9 %copy-start.4 = (bf16[1,256,256]{2,1,0:T(8,128)(2,1)S(1)}, bf16[1,256,256]{2,1,0:T(8,128)(2,1)}, u32[]{:S(2)}) copy-start(bf16[1,256,256]{2,1,0:T(8,128)(2,1)} %param.9) | copy-start | bytes 393220
  163.6 58.3 %collective-permute-start.8 = (bf16[256,1024]{0,1:T(8,128)(2,1)S(1)}, bf16[256,1024]{0,1:T(8,128)(2,1)}, u32[]{:S(2)}, u32[]{:S(2)}) collective-permute-start(bf16[256,1024]{0,1:T(8,128)(2,1)S(1)} %bitcast.119), channel_id=1, source_target_pairs={{0,16},{16,0},{1,17},{17,1},{2,18},{18,2},{3,19},{19,3},{4,20},{20... | collective-permute-start | bytes 1572872 | tf_op jit(solution)/shard_map/ppermute | solution.py:16
  217.9 0.8 copy-start.3
where the time goes:
time: 226 us; the launch traced here: 225 us
  waiting for transfers between devices  154 us (68%)
  starting transfers between devices  52.3 us (23%)
  matrix products  15 us (7%)
  local copies, waits for them, and re-layouts  3.52 us (2%)
    ppermute x9, waiting for transfers between devices, from_partner(): return lax.ppermute(block, axis, route)  111 us
    ppermute x4, waiting for transfers between devices, from_behind(): return lax.ppermute(shard, axis, pairs)  42.8 us
    ppermute x9, starting transfers between devices, from_partner(): return lax.ppermute(block, axis, route)  42.1 us
    dot_general x24, matrix products, mixing(): return jnp.dot(mats, vectors, preferred_element_type=jnp.float32)  15 us
    ppermute x4, starting transfers between devices, from_behind(): return lax.ppermute(shard, axis, pairs)  10.2 us
  transfers between devices with their start and end apart: 13, of which 10 were waited for; matrix products, arithmetic and copies ran while one was open for 5% of the time, Pallas kernels for 0%

commit v1 on v0

v1 whole, which is shorter than its diff:
```python
import jax
import jax.numpy as jnp
from jax import lax
from jax.experimental import pallas as pl
from jax.experimental.pallas import tpu as pltpu
from jax.sharding import PartitionSpec as P


TILE = 256
VMEM = pl.BlockSpec(memory_space=pltpu.VMEM)
SMEM = pl.BlockSpec(memory_space=pltpu.SMEM)


def exchange(block, axis, flip):
    count = lax.axis_size(axis)
    return lax.ppermute(block, axis, [(i, i ^ flip) for i in range(count)])


def from_behind(shard, axis, by):
    devices = lax.axis_size(axis)
    pairs = [(i, i + by) for i in range(devices) if 0 <= i + by < devices]
    return lax.ppermute(shard, axis, pairs)


def mixing(mats, vectors):
    return jnp.dot(mats, vectors, preferred_element_type=jnp.float32)


def rounded(values):
    return values.astype(jnp.bfloat16)


def columns(ref_width):
    return [slice(i, i + TILE) for i in range(0, ref_width, TILE)]


def local(body, outs, ins, products, width=None):
    shapes = [jax.ShapeDtypeStruct(shape, dtype) for shape, dtype in outs]
    moved = sum(x.size * x.dtype.itemsize for x in [*ins, *shapes])

    def spec(x):
        if x.size < 16:
            return SMEM
        if width is None:
            return VMEM
        lead = len(x.shape) - 1
        if x.shape[-1] == width:
            return pl.BlockSpec((*x.shape[:-1], TILE), lambda i: (0,) * lead + (i,))
        return pl.BlockSpec(x.shape, lambda i: (0,) * (lead + 1))

    return pl.pallas_call(
        body,
        out_shape=shapes,
        grid=() if width is None else (width // TILE,),
        in_specs=[spec(x) for x in ins],
        out_specs=[spec(x) for x in shapes],
        compiler_params=pltpu.CompilerParams(vmem_limit_bytes=8 << 20),
        cost_estimate=pl.CostEstimate(flops=products * 2**25, bytes_accessed=moved, transcendentals=0),
    )(*ins)


def near_products(live, tiles, sources, steps):
    block = sources[...]
    steps[0] = rounded(live[0, 1] * mixing(tiles[0, 1], block))
    steps[1] = rounded(live[0, 3] * mixing(tiles[0, 3], block))


def near_meet(core, live, tiles, sources, met, down, up):
    block = sources[...]
    lowest = live[0, 0] * mixing(tiles[0, 0], block)
    highest = live[0, 4] * mixing(tiles[0, 4], block)
    first = core[0] == 0
    down[...] = rounded(lowest + jnp.where(first, 0.0, met[0].astype(jnp.float32)))
    up[...] = rounded(highest + jnp.where(first, met[1].astype(jnp.float32), 0.0))


def pair_ready(near, at_side, one, other, ready_one, ready_other, across, first):
    first[...] = near[0, 0]
    across[...] = rounded(mixing(near[1, 1], at_side[0]))
    for cols in columns(one.shape[1]):
        ready_one[:, cols] = mixing(near[0, 1], one[:, cols])
        ready_other[:, cols] = mixing(near[1, 0], rounded(mixing(near[0, 1], other[:, cols])))


def pair_send(mat, ready, arrived, sent):
    for cols in columns(arrived.shape[1]):
        sent[:, cols] = rounded(ready[:, cols] + mixing(mat[...], arrived[:, cols]))


def finish_base(level):
    def body(core, live, transfers, leaf_out, at_side, tiles, one, low, other, side, sources, met, above, beneath, base_one, base_other, out_second):
        out = leaf_out[0]
        first, second = transfers[0, level], transfers[0, level + 1]
        out_second[...] = rounded(mixing(out, second[1]))
        half = one.shape[1]
        for cols in columns(half):
            mine = rounded(mixing(first[0], one[:, cols]) + mixing(first[1], low[:, cols]))
            base_one[:, cols] = mixing(out, rounded(mixing(second[0], mine)))
            own = mixing(second[0], rounded(mixing(first[0], other[:, cols])))
            own = own + mixing(second[1], rounded(mixing(at_side[1], side[:, cols])))
            base_other[:, cols] = mixing(out, rounded(own))
        for base, start in ((base_one, 0), (base_other, half)):
            for cols in columns(half):
                at = slice(start + cols.start, start + cols.stop)
                near = live[0, 2] * mixing(tiles[0, 2], sources[:, at])
                near = near + above[:, at].astype(jnp.float32) + beneath[:, at].astype(jnp.float32)
                step = jnp.where(core[0] == 0, met[0, :, at], met[1, :, at])
                base[:, cols] = base[:, cols] + near + step.astype(jnp.float32)

    return body


def finish(out_second, leaf_out, base_one, passed, base_other, added, result):
    half = passed.shape[1]
    for cols in columns(half):
        result[:, cols] = rounded(base_one[:, cols] + mixing(out_second[...], passed[:, cols]))
        at = slice(half + cols.start, half + cols.stop)
        result[:, at] = rounded(base_other[:, cols] + mixing(leaf_out[0], added[:, cols]))


def shards(sources, leaf_in, transfers, leaf_out, tile_mats, tile_list):
    levels_high = lax.axis_size("row").bit_length() - 1
    levels_low = lax.axis_size("col").bit_length() - 1
    hops = [("row", 1 << bit) for bit in range(levels_high)]
    hops += [("col", 1 << bit) for bit in range(levels_low)]
    last = len(hops) - 1
    rank, vecs = sources.shape
    half = vecs // 2
    bf16, f32 = jnp.bfloat16, jnp.float32
    live = tile_list.astype(f32)
    core = lax.axis_index("col").reshape(1) % 2

    coeffs = rounded(mixing(leaf_in[0], sources))

    low_bit, high_bit = hops[last - 1][1], hops[last][1]
    side_bit = low_bit ^ high_bit
    near = exchange(transfers[0, last - 1 :], "col", low_bit)
    at_side = exchange(jnp.stack([transfers[0, last - 1, 0], near[0, 1]]), "col", side_bit)

    (steps,) = local(near_products, [((2, rank, vecs), bf16)], [live, tile_mats, sources], 8, vecs)
    met = exchange(steps, "col", 1)
    down, up = local(near_meet, [((rank, vecs), bf16)] * 2, [core, live, tile_mats, sources, met], 8, vecs)
    above = from_behind(up, "col", 2)
    beneath = from_behind(down, "col", -2)

    for level in range(last - 1):
        axis, flip = hops[level]
        partner = exchange(coeffs, axis, flip)
        coeffs = rounded(mixing(transfers[0, level, 0], coeffs) + mixing(transfers[0, level, 1], partner))

    one, other = coeffs[:, :half], coeffs[:, half:]
    low = exchange(one, "col", low_bit)
    side = exchange(other, "col", side_bit)
    ready_one, ready_other, across, first = local(
        pair_ready,
        [((rank, half), f32), ((rank, half), f32), ((rank, rank), bf16), ((rank, rank), bf16)],
        [near, at_side, one, other],
        7,
    )
    (passed,) = local(pair_send, [((rank, half), bf16)], [first, ready_one, low], 1)
    passed = exchange(passed, "col", side_bit)
    (part,) = local(pair_send, [((rank, half), bf16)], [across, ready_other, side], 1)
    added = exchange(part, "col", low_bit)
    base_one, base_other, out_second = local(
        finish_base(last - 1),
        [((rank, half), f32), ((rank, half), f32), ((rank, rank), bf16)],
        [core, live, transfers, leaf_out, at_side, tile_mats, one, low, other, side, sources, met, above, beneath],
        23,
    )
    (result,) = local(finish, [((rank, vecs), bf16)], [out_second, leaf_out, base_one, passed, base_other, added], 4)
    return result


def solution(mesh):
    return jax.shard_map(
        shards,
        mesh=mesh,
        in_specs=(
            P(("row", "col"), None),
            P(("row", "col"), None, None),
            P(("row", "col"), None, None, None, None),
            P(("row", "col"), None, None),
            P(("row", "col"), None, None, None),
            P(("row", "col"), None),
        ),
        out_specs=P(("row", "col"), None),
        check_vma=False,
    )
```

time: 226 us -> 237 us (1.049)
  the two profiles are of different devices: /device:TPU:96 before, /device:TPU:74 now
where the time goes in v1:
time: 237 us; the launch traced here: 236 us
  waiting for transfers between devices  114 us (48%)
  starting transfers between devices  98.9 us (42%)
  Pallas kernels  11.5 us (5%)
  matrix products  9.85 us (4%)
    ppermute x14, waiting for transfers between devices, exchange(): return lax.ppermute(block, axis, [(i, i ^ flip) for i in range(count)])  114 us
    ppermute x14, starting transfers between devices, exchange(): return lax.ppermute(block, axis, [(i, i ^ flip) for i in range(count)])  89.2 us
    pallas_call x7, Pallas kernels, local(): pl.pallas_call(body, out_shape=shapes, grid=() if width is None else (wid...  11.5 us
    dot_general x15, matrix products, mixing(): return jnp.dot(mats, vectors, preferred_element_type=jnp.float32)  9.85 us
    ppermute x2, starting transfers between devices, from_behind(): return lax.ppermute(shard, axis, pairs)  9.7 us
  transfers between devices with their start and end apart: 16, of which 11 were waited for; matrix products, arithmetic and copies ran while one was open for 3% of the time, Pallas kernels for 4%

profile of v1, /device:TPU:74, one launch (start us, length us, event | category | flops | bytes accessed | tf_op | source)
XLA Modules:
  0.0 236.3 jit_solution(10891603432676620070)
XLA Ops:
  0.0 0.0 copy-start
  0.0 0.9 copy-done
  0.9 1.3 convolution_convert_fusion
  2.3 2.4 %collective-permute-start.2 = (bf16[256,1024]{1,0:T(8,128)(2,1)S(1)}, bf16[256,1024]{1,0:T(8,128)(2,1)S(1)}, u32[]{:S(2)}, u32[]{:S(2)}) collective-permute-start(bf16[256,1024]{1,0:T(8,128)(2,1)S(1)} %convolution_convert_fusion), channel_id=1, source_target_pairs={{0,32},{32,0},{64,96},{96,64},{128,160},{160,128},{192,224},{224,1... | collective-permute-start | bytes 1572872 | tf_op jit(solution)/shard_map/ppermute | solution.py:16
  4.7 1.3 fusion.27
  6.0 11.8 %collective-permute-done.2 = bf16[256,1024]{1,0:T(8,128)(2,1)S(1)} collective-permute-done((bf16[256,1024]{1,0:T(8,128)(2,1)S(1)}, bf16[256,1024]{1,0:T(8,128)(2,1)S(1)}, u32[]{:S(2)}, u32[]{:S(2)}) %collective-permute-start.2) | collective-permute-done | bytes 524320 | tf_op jit(solution)/shard_map/ppermute | solution.py:16
  17.8 0.0 copy-done.1
  17.8 0.4 fusion
  18.2 4.0 %collective-permute-start.3 = (bf16[256,1024]{0,1:T(8,128)(2,1)S(1)}, bf16[256,1024]{0,1:T(8,128)(2,1)S(1)}, u32[]{:S(2)}, u32[]{:S(2)}) collective-permute-start(bf16[256,1024]{0,1:T(8,128)(2,1)S(1)} %bitcast.76), channel_id=1, source_target_pairs={{0,64},{32,96},{64,0},{96,32},{128,192},{160,224},{192,128},{224,1... | collective-permute-start | bytes 1572872 | tf_op jit(solution)/shard_map/ppermute | solution.py:16
  22.2 0.3 fusion.24
  22.6 11.8 %collective-permute-done.3 = bf16[256,1024]{0,1:T(8,128)(2,1)S(1)} collective-permute-done((bf16[256,1024]{0,1:T(8,128)(2,1)S(1)}, bf16[256,1024]{0,1:T(8,128)(2,1)S(1)}, u32[]{:S(2)}, u32[]{:S(2)}) %collective-permute-start.3) | collective-permute-done | bytes 524320 | tf_op jit(solution)/shard_map/ppermute | solution.py:16
  34.4 0.3 fusion.1
  34.7 2.4 collective-permute-start.4
  37.1 0.3 fusion.21
  37.4 11.2 %collective-permute-done.4 = bf16[256,1024]{0,1:T(8,128)(2,1)S(1)} collective-permute-done((bf16[256,1024]{0,1:T(8,128)(2,1)S(1)}, bf16[256,1024]{0,1:T(8,128)(2,1)S(1)}, u32[]{:S(2)}, u32[]{:S(2)}) %collective-permute-start.4) | collective-permute-done | bytes 524320 | tf_op jit(solution)/shard_map/ppermute | solution.py:16
  48.6 0.3 fusion.2
  48.9 4.2 %collective-permute-start.5 = (bf16[256,1024]{0,1:T(8,128)(2,1)S(1)}, bf16[256,1024]{0,1:T(8,128)(2,1)S(1)}, u32[]{:S(2)}, u32[]{:S(2)}) collective-permute-start(bf16[256,1024]{0,1:T(8,128)(2,1)S(1)} %bitcast.78), channel_id=1, source_target_pairs={{0,256},{32,288},{64,320},{96,352},{128,384},{160,416},{192,448},{... | collective-permute-start | bytes 1572872 | tf_op jit(solution)/shard_map/ppermute | solution.py:16
  53.1 0.3 fusion.18
  53.4 10.0 %collective-permute-done.5 = bf16[256,1024]{0,1:T(8,128)(2,1)S(1)} collective-permute-done((bf16[256,1024]{0,1:T(8,128)(2,1)S(1)}, bf16[256,1024]{0,1:T(8,128)(2,1)S(1)}, u32[]{:S(2)}, u32[]{:S(2)}) %collective-permute-start.5) | collective-permute-done | bytes 524320 | tf_op jit(solution)/shard_map/ppermute | solution.py:16
  63.4 0.3 fusion.3
  63.7 0.0 copy-start.6
  63.7 0.0 copy-start.2
  63.7 0.0 copy-start.3
  63.8 2.1 collective-permute-start.6
  65.8 0.3 fusion.15
  66.1 1.5 collective-permute-done.6
  67.7 1.1 fusion.4
  68.8 3.8 %collective-permute-start.7 = (bf16[256,1024]{0,1:T(8,128)(2,1)}, bf16[256,1024]{0,1:T(8,128)(2,1)}, u32[]{:S(2)}, u32[]{:S(2)}) collective-permute-start(bf16[256,1024]{0,1:T(8,128)(2,1)} %bitcast.20), channel_id=1, source_target_pairs={{0,2},{1,3},{2,0},{3,1},{4,6},{5,7},{6,4},{7,5},{8,10},{9,11},{10,... | collective-permute-start | bytes 1572872 | tf_op jit(solution)/shard_map/ppermute | solution.py:16
  72.7 0.8 slice_bitcast_fusion
  73.5 9.1 %collective-permute-start = (bf16[2,2,256,256]{3,2,1,0:T(8,128)(2,1)}, bf16[2,2,256,256]{3,2,1,0:T(8,128)(2,1)S(1)}, u32[]{:S(2)}, u32[]{:S(2)}) collective-permute-start(bf16[2,2,256,256]{3,2,1,0:T(8,128)(2,1)} %slice_bitcast_fusion), channel_id=1, source_target_pairs={{0,8},{1,9},{2,10},{3,11},{4,12},{5,13},{6,14},{7,15},{8,0},{9,1},... | collective-permute-start | bytes 1572872 | tf_op jit(solution)/shard_map/ppermute | solution.py:16
  82.6 0.0 copy-done.6
  82.6 2.8 %shard_map.64 = bf16[2,256,1024]{2,1,0:T(8,128)(2,1)} custom-call(f32[1,5]{1,0:T(1,128)S(1)} %convert_element_type.48.live, bf16[1,5,256,256]{3,2,1,0:T(8,128)(2,1)S(1)} %copy-done.3, bf16[256,1024]{1,0:T(8,128)(2,1)S(1)} %copy-done.2), custom_call_target="tpu_custom_call" | custom-call | flops 268435456 | bytes 2228244 | tf_op jit(solution)/shard_map/pallas_call | solution.py:51
  85.4 1.9 collective-permute-start.11
  87.3 0.0 copy-start.4
  87.4 1.4 fusion.12
  88.8 18.9 %collective-permute-done.7 = bf16[256,1024]{0,1:T(8,128)(2,1)} collective-permute-done((bf16[256,1024]{0,1:T(8,128)(2,1)}, bf16[256,1024]{0,1:T(8,128)(2,1)}, u32[]{:S(2)}, u32[]{:S(2)}) %collective-permute-start.7) | collective-permute-done | bytes 524320 | tf_op jit(solution)/shard_map/ppermute | solution.py:16
  107.7 1.4 fusion.5
  109.1 1.9 collective-permute-start.8
  111.0 7.3 %collective-permute-done.near = bf16[2,2,256,256]{3,2,1,0:T(8,128)(2,1)S(1)} collective-permute-done((bf16[2,2,256,256]{3,2,1,0:T(8,128)(2,1)}, bf16[2,2,256,256]{3,2,1,0:T(8,128)(2,1)S(1)}, u32[]{:S(2)}, u32[]{:S(2)}) %collective-permute-start) | collective-permute-done | bytes 524320 | tf_op jit(solution)/shard_map/ppermute | solution.py:16
  118.4 14.1 %collective-permute-start.1 = (bf16[2,256,256]{2,1,0:T(8,128)(2,1)S(1)}, bf16[2,256,256]{2,1,0:T(8,128)(2,1)S(1)}, u32[]{:S(2)}, u32[]{:S(2)}) collective-permute-start(bf16[2,256,256]{2,1,0:T(8,128)(2,1)S(1)} %pad_maximum_fusion), channel_id=1, source_target_pairs={{0,24},{1,25},{2,26},{3,27},{4,28},{5,29},{6,30},{7,31},{8,16},{9,... | collective-permute-start | bytes 786440 | tf_op jit(solution)/shard_map/ppermute | solution.py:16
  132.5 0.0 collective-permute-done.11.met
  132.5 2.8 %shard_map.65 = (bf16[256,1024]{1,0:T(8,128)(2,1)S(1)}, bf16[256,1024]{1,0:T(8,128)(2,1)S(1)}) custom-call(s32[1]{0:T(128)S(6)} %select_n.7.core, f32[1,5]{1,0:T(1,128)S(1)} %convert_element_type.48.live, bf16[1,5,256,256]{3,2,1,0:T(8,128)(2,1)S(1)} %copy-done.4, bf16[256,1024]{1,0:T(8,128)(2,1)S(1)} %copy-done.2, ...), custom_call_target="tpu_custom_call" | custom-call | flops 268435456 | bytes 3276824 | tf_op jit(solution)/shard_map/pallas_call | solution.py:51
  135.3 7.8 %collective-permute-start.12 = (bf16[256,1024]{1,0:T(8,128)(2,1)S(1)}, bf16[256,1024]{1,0:T(8,128)(2,1)S(1)}, u32[]{:S(2)}, u32[]{:S(2)}) collective-permute-start(bf16[256,1024]{1,0:T(8,128)(2,1)S(1)} %get-tuple-element.14), channel_id=1, source_target_pairs={{0,2},{1,3},{2,4},{3,5},{4,6},{5,7},{6,8},{7,9},{8,10},{9,11},{10,... | collective-permute-start | bytes 1572872 | tf_op jit(solution)/shard_map/ppermute | solution.py:22
  143.1 1.9 collective-permute-start.13
  145.0 0.3 fusion.9
  145.4 7.6 %collective-permute-done.8 = bf16[256,1024]{0,1:T(8,128)(2,1)S(1)} collective-permute-done((bf16[256,1024]{0,1:T(8,128)(2,1)S(1)}, bf16[256,1024]{0,1:T(8,128)(2,1)S(1)}, u32[]{:S(2)}, u32[]{:S(2)}) %collective-permute-start.8) | collective-permute-done | bytes 524320 | tf_op jit(solution)/shard_map/ppermute | solution.py:16
  153.0 0.3 fusion.7
  153.3 0.0 copy-start.5
  153.4 2.4 collective-permute-start.10
  155.7 13.4 %collective-permute-start.9 = (bf16[256,512]{1,0:T(8,128)(2,1)S(1)}, bf16[256,512]{1,0:T(8,128)(2,1)S(1)}, u32[]{:S(2)}, u32[]{:S(2)}) collective-permute-start(bf16[256,512]{1,0:T(8,128)(2,1)S(1)} %get-tuple-element.24.one), channel_id=1, source_target_pairs={{0,8},{1,9},{2,10},{3,11},{4,12},{5,13},{6,14},{7,15},{8,0},{9,1},... | collective-permute-start | bytes 786440 | tf_op jit(solution)/shard_map/ppermute | solution.py:16
  169.2 0.0 collective-permute-done.1.at_side
  169.2 0.7 shard_map.67
  169.9 22.5 %collective-permute-done.10.side.arrived = bf16[256,512]{1,0:T(8,128)(2,1)S(1)} collective-permute-done((bf16[256,512]{1,0:T(8,128)(2,1)S(1)}, bf16[256,512]{1,0:T(8,128)(2,1)S(1)}, u32[]{:S(2)}, u32[]{:S(2)}) %collective-permute-start.10) | collective-permute-done | bytes 262176 | tf_op jit(solution)/shard_map/ppermute | solution.py:16
  192.3 0.2 shard_map.69
  192.6 25.6 %collective-permute-start.15 = (bf16[256,512]{1,0:T(8,128)(2,1)S(1)}, bf16[256,512]{1,0:T(8,128)(2,1)S(1)}, u32[]{:S(2)}, u32[]{:S(2)}) collective-permute-start(bf16[256,512]{1,0:T(8,128)(2,1)S(1)} %shard_map.69), channel_id=1, source_target_pairs={{0,8},{1,9},{2,10},{3,11},{4,12},{5,13},{6,14},{7,15},{8,0},{9,1},... | collective-permute-start | bytes 786440 | tf_op jit(solution)/shard_map/ppermute | solution.py:16
  218.2 0.0 collective-permute-done.9.low.arrived
  218.2 0.2 shard_map.68
  218.4 1.9 collective-permute-start.14
  220.4 0.0 collective-permute-done.12.above
  220.4 0.0 collective-permute-done.13.beneath
  220.4 3.7 %shard_map.66 = (f32[256,512]{1,0:T(8,128)S(1)}, f32[256,512]{1,0:T(8,128)S(1)}, bf16[256,256]{1,0:T(8,128)(2,1)S(1)}) custom-call(s32[1]{0:T(128)S(6)} %select_n.7.core, f32[1,5]{1,0:T(1,128)S(1)} %convert_element_type.48.live, bf16[1,9,2,256,256]{4,3,2,1,0:T(8,128)(2,1)S(1)} %copy-done.1, bf16[1,256,256]{2,1,0:T(8,128)(2,1)S(1)} %copy-done.5, ...), custom_call_target="tpu_custom_call" | custom-call | flops 771751936 | bytes 8257560 | tf_op jit(solution)/shard_map/pallas_call | solution.py:51
  224.0 2.6 %collective-permute-done.15.added = bf16[256,512]{1,0:T(8,128)(2,1)S(1)} collective-permute-done((bf16[256,512]{1,0:T(8,128)(2,1)S(1)}, bf16[256,512]{1,0:T(8,128)(2,1)S(1)}, u32[]{:S(2)}, u32[]{:S(2)}) %collective-permute-start.15) | collective-permute-done | bytes 262176 | tf_op jit(solution)/shard_map/ppermute | solution.py:16
  226.6 8.6 %collective-permute-done.14.passed = bf16[256,512]{1,0:T(8,128)(2,1)S(1)} collective-permute-done((bf16[256,512]{1,0:T(8,128)(2,1)S(1)}, bf16[256,512]{1,0:T(8,128)(2,1)S(1)}, u32[]{:S(2)}, u32[]{:S(2)}) %collective-permute-start.14) | collective-permute-done | bytes 262176 | tf_op jit(solution)/shard_map/ppermute | solution.py:16
  235.2 1.1 shard_map.70
  (10 shorter events, 0.1 us)
Async XLA Ops:
  0.0 0.9 copy-start
  0.0 17.8 %copy-start.1 = (bf16[1,9,2,256,256]{4,3,2,1,0:T(8,128)(2,1)S(1)}, bf16[1,9,2,256,256]{4,3,2,1,0:T(8,128)(2,1)}, u32[]{:S(2)}) copy-start(bf16[1,9,2,256,256]{4,3,2,1,0:T(8,128)(2,1)} %transfers.1) | copy-start | bytes 7077892
  2.3 15.6 %collective-permute-start.2 = (bf16[256,1024]{1,0:T(8,128)(2,1)S(1)}, bf16[256,1024]{1,0:T(8,128)(2,1)S(1)}, u32[]{:S(2)}, u32[]{:S(2)}) collective-permute-start(bf16[256,1024]{1,0:T(8,128)(2,1)S(1)} %convolution_convert_fusion), channel_id=1, source_target_pairs={{0,32},{32,0},{64,96},{96,64},{128,160},{160,128},{192,224},{224,1... | collective-permute-start | bytes 1572872 | tf_op jit(solution)/shard_map/ppermute | solution.py:16
  18.2 16.2 %collective-permute-start.3 = (bf16[256,1024]{0,1:T(8,128)(2,1)S(1)}, bf16[256,1024]{0,1:T(8,128)(2,1)S(1)}, u32[]{:S(2)}, u32[]{:S(2)}) collective-permute-start(bf16[256,1024]{0,1:T(8,128)(2,1)S(1)} %bitcast.76), channel_id=1, source_target_pairs={{0,64},{32,96},{64,0},{96,32},{128,192},{160,224},{192,128},{224,1... | collective-permute-start | bytes 1572872 | tf_op jit(solution)/shard_map/ppermute | solution.py:16
  34.7 13.9 %collective-permute-start.4 = (bf16[256,1024]{0,1:T(8,128)(2,1)S(1)}, bf16[256,1024]{0,1:T(8,128)(2,1)S(1)}, u32[]{:S(2)}, u32[]{:S(2)}) collective-permute-start(bf16[256,1024]{0,1:T(8,128)(2,1)S(1)} %bitcast.77), channel_id=1, source_target_pairs={{0,128},{32,160},{64,192},{96,224},{128,0},{160,32},{192,64},{224,... | collective-permute-start | bytes 1572872 | tf_op jit(solution)/shard_map/ppermute | solution.py:16
  48.9 14.5 %collective-permute-start.5 = (bf16[256,1024]{0,1:T(8,128)(2,1)S(1)}, bf16[256,1024]{0,1:T(8,128)(2,1)S(1)}, u32[]{:S(2)}, u32[]{:S(2)}) collective-permute-start(bf16[256,1024]{0,1:T(8,128)(2,1)S(1)} %bitcast.78), channel_id=1, source_target_pairs={{0,256},{32,288},{64,320},{96,352},{128,384},{160,416},{192,448},{... | collective-permute-start | bytes 1572872 | tf_op jit(solution)/shard_map/ppermute | solution.py:16
  63.7 18.8 %copy-start.6 = (s32[1,5]{1,0:T(1,128)S(1)}, s32[1,5]{1,0:T(1,128)}, u32[]{:S(2)}) copy-start(s32[1,5]{1,0:T(1,128)} %param.11) | copy-start | bytes 64
  63.7 18.9 %copy-start.2 = (bf16[256,1024]{1,0:T(8,128)(2,1)S(1)}, bf16[256,1024]{1,0:T(8,128)(2,1)}, u32[]{:S(2)}) copy-start(bf16[256,1024]{1,0:T(8,128)(2,1)} %sources.5) | copy-start | bytes 1572868
  63.7 18.9 %copy-start.3 = (bf16[1,5,256,256]{3,2,1,0:T(8,128)(2,1)S(1)}, bf16[1,5,256,256]{3,2,1,0:T(8,128)(2,1)}, u32[]{:S(2)}) copy-start(bf16[1,5,256,256]{3,2,1,0:T(8,128)(2,1)} %tiles.5) | copy-start | bytes 1966084
  63.8 3.9 %collective-permute-start.6 = (bf16[256,1024]{0,1:T(8,128)(2,1)S(1)}, bf16[256,1024]{0,1:T(8,128)(2,1)S(1)}, u32[]{:S(2)}, u32[]{:S(2)}) collective-permute-start(bf16[256,1024]{0,1:T(8,128)(2,1)S(1)} %bitcast.79), channel_id=1, source_target_pairs={{0,1},{1,0},{2,3},{3,2},{4,5},{5,4},{6,7},{7,6},{8,9},{9,8},{10,11... | collective-permute-start | bytes 1572872 | tf_op jit(solution)/shard_map/ppermute | solution.py:16
  68.8 38.9 %collective-permute-start.7 = (bf16[256,1024]{0,1:T(8,128)(2,1)}, bf16[256,1024]{0,1:T(8,128)(2,1)}, u32[]{:S(2)}, u32[]{:S(2)}) collective-permute-start(bf16[256,1024]{0,1:T(8,128)(2,1)} %bitcast.20), channel_id=1, source_target_pairs={{0,2},{1,3},{2,0},{3,1},{4,6},{5,7},{6,4},{7,5},{8,10},{9,11},{10,... | collective-permute-start | bytes 1572872 | tf_op jit(solution)/shard_map/ppermute | solution.py:16
  73.5 44.8 %collective-permute-start = (bf16[2,2,256,256]{3,2,1,0:T(8,128)(2,1)}, bf16[2,2,256,256]{3,2,1,0:T(8,128)(2,1)S(1)}, u32[]{:S(2)}, u32[]{:S(2)}) collective-permute-start(bf16[2,2,256,256]{3,2,1,0:T(8,128)(2,1)} %slice_bitcast_fusion), channel_id=1, source_target_pairs={{0,8},{1,9},{2,10},{3,11},{4,12},{5,13},{6,14},{7,15},{8,0},{9,1},... | collective-permute-start | bytes 1572872 | tf_op jit(solution)/shard_map/ppermute | solution.py:16
  85.4 47.1 %collective-permute-start.11 = (bf16[2,256,1024]{2,1,0:T(8,128)(2,1)}, bf16[2,256,1024]{2,1,0:T(8,128)(2,1)}, u32[]{:S(2)}, u32[]{:S(2)}) collective-permute-start(bf16[2,256,1024]{2,1,0:T(8,128)(2,1)} %shard_map.64), channel_id=1, source_target_pairs={{0,1},{1,0},{2,3},{3,2},{4,5},{5,4},{6,7},{7,6},{8,9},{9,8},{10,11... | collective-permute-start | bytes 3145736 | tf_op jit(solution)/shard_map/ppermute | solution.py:16
  87.3 45.1 %copy-start.4 = (bf16[1,5,256,256]{3,2,1,0:T(8,128)(2,1)S(1)}, bf16[1,5,256,256]{3,2,1,0:T(8,128)(2,1)}, u32[]{:S(2)}) copy-start(bf16[1,5,256,256]{3,2,1,0:T(8,128)(2,1)} %tiles.5) | copy-start | bytes 1966084
  109.1 43.9 %collective-permute-start.8 = (bf16[256,1024]{0,1:T(8,128)(2,1)S(1)}, bf16[256,1024]{0,1:T(8,128)(2,1)S(1)}, u32[]{:S(2)}, u32[]{:S(2)}) collective-permute-start(bf16[256,1024]{0,1:T(8,128)(2,1)S(1)} %bitcast.75), channel_id=1, source_target_pairs={{0,4},{1,5},{2,6},{3,7},{4,0},{5,1},{6,2},{7,3},{8,12},{9,13},{10,... | collective-permute-start | bytes 1572872 | tf_op jit(solution)/shard_map/ppermute | solution.py:16
  118.4 50.8 %collective-permute-start.1 = (bf16[2,256,256]{2,1,0:T(8,128)(2,1)S(1)}, bf16[2,256,256]{2,1,0:T(8,128)(2,1)S(1)}, u32[]{:S(2)}, u32[]{:S(2)}) collective-permute-start(bf16[2,256,256]{2,1,0:T(8,128)(2,1)S(1)} %pad_maximum_fusion), channel_id=1, source_target_pairs={{0,24},{1,25},{2,26},{3,27},{4,28},{5,29},{6,30},{7,31},{8,16},{9,... | collective-permute-start | bytes 786440 | tf_op jit(solution)/shard_map/ppermute | solution.py:16
  135.3 85.1 %collective-permute-start.12 = (bf16[256,1024]{1,0:T(8,128)(2,1)S(1)}, bf16[256,1024]{1,0:T(8,128)(2,1)S(1)}, u32[]{:S(2)}, u32[]{:S(2)}) collective-permute-start(bf16[256,1024]{1,0:T(8,128)(2,1)S(1)} %get-tuple-element.14), channel_id=1, source_target_pairs={{0,2},{1,3},{2,4},{3,5},{4,6},{5,7},{6,8},{7,9},{8,10},{9,11},{10,... | collective-permute-start | bytes 1572872 | tf_op jit(solution)/shard_map/ppermute | solution.py:22
  143.1 77.3 %collective-permute-start.13 = (bf16[256,1024]{1,0:T(8,128)(2,1)S(1)}, bf16[256,1024]{1,0:T(8,128)(2,1)S(1)}, u32[]{:S(2)}, u32[]{:S(2)}) collective-permute-start(bf16[256,1024]{1,0:T(8,128)(2,1)S(1)} %get-tuple-element.15), channel_id=1, source_target_pairs={{2,0},{3,1},{4,2},{5,3},{6,4},{7,5},{8,6},{9,7},{10,8},{11,9},{12,... | collective-permute-start | bytes 1572872 | tf_op jit(solution)/shard_map/ppermute | solution.py:22
  153.3 67.1 %copy-start.5 = (bf16[1,256,256]{2,1,0:T(8,128)(2,1)S(1)}, bf16[1,256,256]{2,1,0:T(8,128)(2,1)}, u32[]{:S(2)}) copy-start(bf16[1,256,256]{2,1,0:T(8,128)(2,1)} %leaf_out.3) | copy-start | bytes 393220
  153.4 39.0 %collective-permute-start.10 = (bf16[256,512]{1,0:T(8,128)(2,1)S(1)}, bf16[256,512]{1,0:T(8,128)(2,1)S(1)}, u32[]{:S(2)}, u32[]{:S(2)}) collective-permute-start(bf16[256,512]{1,0:T(8,128)(2,1)S(1)} %get-tuple-element.23.other), channel_id=1, source_target_pairs={{0,24},{1,25},{2,26},{3,27},{4,28},{5,29},{6,30},{7,31},{8,16},{9,... | collective-permute-start | bytes 786440 | tf_op jit(solution)/shard_map/ppermute | solution.py:16
  155.7 62.5 %collective-permute-start.9 = (bf16[256,512]{1,0:T(8,128)(2,1)S(1)}, bf16[256,512]{1,0:T(8,128)(2,1)S(1)}, u32[]{:S(2)}, u32[]{:S(2)}) collective-permute-start(bf16[256,512]{1,0:T(8,128)(2,1)S(1)} %get-tuple-element.24.one), channel_id=1, source_target_pairs={{0,8},{1,9},{2,10},{3,11},{4,12},{5,13},{6,14},{7,15},{8,0},{9,1},... | collective-permute-start | bytes 786440 | tf_op jit(solution)/shard_map/ppermute | solution.py:16
  192.6 34.1 %collective-permute-start.15 = (bf16[256,512]{1,0:T(8,128)(2,1)S(1)}, bf16[256,512]{1,0:T(8,128)(2,1)S(1)}, u32[]{:S(2)}, u32[]{:S(2)}) collective-permute-start(bf16[256,512]{1,0:T(8,128)(2,1)S(1)} %shard_map.69), channel_id=1, source_target_pairs={{0,8},{1,9},{2,10},{3,11},{4,12},{5,13},{6,14},{7,15},{8,0},{9,1},... | collective-permute-start | bytes 786440 | tf_op jit(solution)/shard_map/ppermute | solution.py:16
  218.4 16.8 %collective-permute-start.14 = (bf16[256,512]{1,0:T(8,128)(2,1)S(1)}, bf16[256,512]{1,0:T(8,128)(2,1)S(1)}, u32[]{:S(2)}, u32[]{:S(2)}) collective-permute-start(bf16[256,512]{1,0:T(8,128)(2,1)S(1)} %shard_map.68), channel_id=1, source_target_pairs={{0,24},{1,25},{2,26},{3,27},{4,28},{5,29},{6,30},{7,31},{8,16},{9,... | collective-permute-start | bytes 786440 | tf_op jit(solution)/shard_map/ppermute | solution.py:16
